TPU v7x, 128 devices: a whole 4x4x4 slice. The times are simulated.
128 devices in a mesh: seq: 32 (over x, y, core), tp: 4 (over z).
Axes of the slice: x: 4, y: 4, z: 4, core: 2. Of those that a mesh axis runs over, the one named last changes fastest.
Arguments:
- states_in: bfloat16 [8192, 2048], P('seq'), may hold values from -7 to 7
- lengths: int32 [4], replicated, may hold values from 1 to 64, 128 in all
- attn_gain: float32 [2048], replicated, may hold values from 0.5 to 1.5
- w_query: bfloat16 [2048, 2048], P(None, 'tp'), may hold values from -0.125 to 0.125
- w_key: bfloat16 [2048, 2048], P(None, 'tp'), may hold values from -0.088388348 to 0.088388348
- w_value: bfloat16 [2048, 4096], P(None, 'tp'), may hold values from -0.125 to 0.125
- w_gate: bfloat16 [2048, 4096], P(None, 'tp'), may hold values from -0.125 to 0.125
- w_beta: bfloat16 [2048, 16], P(None, 'tp'), may hold values from -1 to 1
- w_alpha: bfloat16 [2048, 16], P(None, 'tp'), may hold values from -0.125 to 0.125
- decay_rate: float32 [16], P('tp'), may hold values from 4.8828125e-05 to 0.05
- decay_bias: float32 [16], P('tp'), may hold values from -2 to 1
- conv_query: float32 [4, 2048], P(None, 'tp'), may hold values from -3 to 3
- conv_key: float32 [4, 2048], P(None, 'tp'), may hold values from -3 to 3
- conv_value: float32 [4, 4096], P(None, 'tp'), may hold values from -4.5 to 4.5
- out_gain: float32 [256], replicated, may hold values from 0.5 to 1.5
- w_out: bfloat16 [4096, 2048], P('tp'), may hold values from -0.09375 to 0.09375
- final_gain: float32 [2048], replicated, may hold values from 0.5 to 1.5
- w_head: bfloat16 [2048, 32000], P(None, ('seq', 'tp')), may hold values from -0.41992188 to 0.41992188
Outputs:
- hidden: bfloat16 [8192, 2048], P('seq', 'tp')
- block_states: float32 [128, 16, 128, 256], P('seq', 'tp')
- max_logit: float32 [4], replicated
Inputs may be any that keep to these rules, and one draw needn't show every extreme that they name: Prompt lengths are counted in blocks of 64 tokens; they sum to 128 and the longest is 64.
All inputs are finite; a program needn't handle non-finite values.
Results may differ from a plain program's by a relative error of at most 0.0095.
Values may be sent and summed in bfloat16 or wider, within the bound.
No kernel may reach another device: no remote copies, remote signals or barrier semaphores. Data moves between devices by JAX's collectives and lax.ppermute only.
A program may use at most 128 MiB of HBM per device.

v0:
```python
import jax
import jax.numpy as jnp
from jax import lax
from jax.sharding import PartitionSpec as P

CONV = 4
BLOCK_LEN = 64
EPS = 1e-06
HIGH = lax.Precision.HIGHEST


def from_behind(value, axis, steps):
    count = lax.axis_size(axis)
    first, last = (max(0, -steps), min(count, count - steps))
    return lax.ppermute(value, axis, [(source, source + steps) for source in range(first, last)])


def rms_scale(values, gain):
    return values * lax.rsqrt(jnp.mean(values * values, axis=-1, keepdims=True) + EPS) * gain


def unit_rows(values):
    return values * lax.rsqrt(jnp.sum(values * values, axis=-1, keepdims=True) + EPS)


def request_start(positions, offsets, block_len):
    block_ids = positions // block_len
    hits = offsets[None, :] <= block_ids[:, None]
    return block_len * jnp.max(jnp.where(hits, offsets[None, :], 0), axis=1)


def short_conv(extended, positions, start_tok, weight):
    row_count = positions.shape[0]
    tap_count = weight.shape[0]
    running = jnp.zeros((row_count, extended.shape[1]), jnp.float32)
    for tap_index in range(tap_count):
        lag_steps = tap_count - 1 - tap_index
        shifted = extended[tap_index : tap_index + row_count].astype(jnp.float32)
        valid = (positions - lag_steps >= start_tok)[:, None]
        running = running + jnp.where(valid, shifted, 0.0) * weight[tap_index]
    return jax.nn.silu(running)


def block_step(carry_state, block_inputs):
    q_rows, k_rows, v_rows, beta_rows, log_cum, keep_flag = block_inputs
    carry_state = carry_state * keep_flag
    block_len = q_rows.shape[1]
    row_ids = lax.broadcasted_iota(jnp.int32, (block_len, block_len), 0)
    col_ids = lax.broadcasted_iota(jnp.int32, (block_len, block_len), 1)
    on_lower = (row_ids >= col_ids).astype(jnp.float32)
    off_lower = (row_ids > col_ids).astype(jnp.float32)
    log_gap = log_cum[:, :, None] - log_cum[:, None, :]
    decays = jnp.exp(jnp.where(row_ids >= col_ids, log_gap, 0.0)) * on_lower
    growth = jnp.exp(log_cum)
    key_gram = jnp.einsum("hid,hjd->hij", k_rows, k_rows, precision=HIGH)
    system_mat = (
        jnp.eye(block_len, dtype=jnp.float32)
        + beta_rows[:, :, None] * key_gram * decays * off_lower
    )
    carried = jnp.einsum("hid,hde->hie", k_rows, carry_state, precision=HIGH)
    right_side = beta_rows[:, :, None] * (v_rows - growth[:, :, None] * carried)
    pseudo_values = lax.linalg.triangular_solve(
        system_mat, right_side, left_side=True, lower=True, unit_diagonal=True
    )
    scores = jnp.einsum("hid,hjd->hij", q_rows, k_rows, precision=HIGH) * decays
    output = growth[:, :, None] * jnp.einsum("hid,hde->hie", q_rows, carry_state, precision=HIGH)
    output = output + jnp.einsum("hij,hje->hie", scores, pseudo_values, precision=HIGH)
    tail_decay = jnp.exp(log_cum[:, -1:] - log_cum)
    carry_state = jnp.exp(log_cum[:, -1])[:, None, None] * carry_state + jnp.einsum(
        "hjd,hje->hde", k_rows * tail_decay[:, :, None], pseudo_values, precision=HIGH
    )
    return (carry_state, (output, carry_state))


def to_blocks(values, block_count, head_count):
    return values.reshape(block_count, BLOCK_LEN, head_count, -1).transpose(0, 2, 1, 3)


def body(
    states_in,
    lengths,
    attn_gain,
    w_query,
    w_key,
    w_value,
    w_gate,
    w_beta,
    w_alpha,
    decay_rate,
    decay_bias,
    conv_query,
    conv_key,
    conv_value,
    out_gain,
    w_out,
    final_gain,
    w_head,
):
    tok_dev = states_in.shape[0]
    heads_dev = decay_rate.shape[0]
    key_dim = w_query.shape[1] // heads_dev
    value_dim = w_value.shape[1] // heads_dev
    blocks_dev = tok_dev // BLOCK_LEN
    piece_index = lax.axis_index("seq")
    x_float = states_in.astype(jnp.float32)
    normed = rms_scale(x_float, attn_gain).astype(jnp.bfloat16)
    pre_q = jnp.dot(normed, w_query, preferred_element_type=jnp.float32).astype(jnp.bfloat16)
    pre_k = jnp.dot(normed, w_key, preferred_element_type=jnp.float32).astype(jnp.bfloat16)
    pre_v = jnp.dot(normed, w_value, preferred_element_type=jnp.float32).astype(jnp.bfloat16)
    gate_raw = jnp.dot(normed, w_gate, preferred_element_type=jnp.float32)
    beta_all = jax.nn.sigmoid(jnp.dot(normed, w_beta, preferred_element_type=jnp.float32))
    log_decay = -decay_rate * jax.nn.softplus(
        jnp.dot(normed, w_alpha, preferred_element_type=jnp.float32) + decay_bias
    )
    ends = jnp.cumsum(lengths)
    offsets = ends - lengths
    positions = piece_index * tok_dev + jnp.arange(tok_dev, dtype=jnp.int32)
    start_tok = request_start(positions, offsets, BLOCK_LEN)
    local_pre = jnp.concatenate([pre_q, pre_k, pre_v], axis=1)
    prev_edge = from_behind(local_pre[tok_dev - (CONV - 1) :], "seq", 1)
    extended = jnp.concatenate([prev_edge, local_pre], axis=0)
    conv_weights = jnp.concatenate([conv_query, conv_key, conv_value], axis=1)
    conv_all = short_conv(extended, positions, start_tok, conv_weights)
    qk_width = heads_dev * key_dim
    q_heads = unit_rows(conv_all[:, :qk_width].reshape(tok_dev, heads_dev, key_dim)) * key_dim ** (
        -0.5
    )
    k_heads = unit_rows(conv_all[:, qk_width : 2 * qk_width].reshape(tok_dev, heads_dev, key_dim))
    q_blocks = to_blocks(q_heads, blocks_dev, heads_dev)
    k_blocks = to_blocks(k_heads, blocks_dev, heads_dev)
    v_blocks = to_blocks(conv_all[:, 2 * qk_width :], blocks_dev, heads_dev)
    v_augmented = jnp.concatenate(
        [jnp.zeros(v_blocks.shape[:3] + (key_dim,), jnp.float32), v_blocks], axis=3
    )
    beta_blocks = beta_all.reshape(blocks_dev, BLOCK_LEN, heads_dev).transpose(0, 2, 1)
    log_blocks = jnp.cumsum(
        log_decay.reshape(blocks_dev, BLOCK_LEN, heads_dev).transpose(0, 2, 1), axis=2
    )
    block_ids = piece_index * blocks_dev + jnp.arange(blocks_dev, dtype=jnp.int32)
    keep_flags = 1.0 - jnp.max((offsets[None, :] == block_ids[:, None]).astype(jnp.float32), axis=1)
    eye_heads = jnp.broadcast_to(jnp.eye(key_dim, dtype=jnp.float32), (heads_dev, key_dim, key_dim))
    initial = jnp.concatenate(
        [eye_heads, jnp.zeros((heads_dev, key_dim, value_dim), jnp.float32)], axis=2
    )
    final_aug, (out_aug, states_aug) = lax.scan(
        block_step, initial, (q_blocks, k_blocks, v_augmented, beta_blocks, log_blocks, keep_flags)
    )
    lin_map = final_aug[:, :, :key_dim]
    offset_state = final_aug[:, :, key_dim:]

    def relay_turn(turn_index, incoming):
        outgoing = jnp.einsum("hde,hef->hdf", lin_map, incoming, precision=HIGH) + offset_state
        return from_behind(outgoing, "seq", 1)

    incoming = lax.fori_loop(0, lax.axis_size("seq") - 1, relay_turn, jnp.zeros_like(offset_state))
    o_blocks = out_aug[..., key_dim:] + jnp.einsum(
        "bhcd,hde->bhce", out_aug[..., :key_dim], incoming, precision=HIGH
    )
    block_states = (
        jnp.einsum("bhde,hef->bhdf", states_aug[..., :key_dim], incoming, precision=HIGH)
        + states_aug[..., key_dim:]
    )
    o_tokens = o_blocks.transpose(0, 2, 1, 3).reshape(tok_dev, heads_dev, value_dim)
    gated = (
        rms_scale(o_tokens, out_gain) * jax.nn.silu(gate_raw.reshape(tok_dev, heads_dev, value_dim))
    ).astype(jnp.bfloat16)
    partial_out = jnp.dot(
        gated.reshape(tok_dev, heads_dev * value_dim), w_out, preferred_element_type=jnp.float32
    )
    model_width = x_float.shape[1]
    share_cols = model_width // lax.axis_size("tp")
    col_start = lax.axis_index("tp") * share_cols
    last_tok = ends * BLOCK_LEN - 1
    picker = (last_tok[:, None] == positions[None, :]).astype(jnp.bfloat16)
    summed = lax.psum(partial_out, "tp")
    hidden_full = (x_float + summed).astype(jnp.bfloat16)
    hidden = lax.dynamic_slice_in_dim(hidden_full, col_start, share_cols, 1)
    picked = jnp.dot(picker, hidden_full, preferred_element_type=jnp.float32)
    last_rows = lax.psum(picked.astype(jnp.bfloat16), "seq").astype(jnp.float32)
    final = rms_scale(last_rows, final_gain).astype(jnp.bfloat16)
    logits = jnp.dot(final, w_head, preferred_element_type=jnp.float32)
    max_logit = lax.pmax(jnp.max(logits, axis=1), ("seq", "tp"))
    return (hidden, block_states, max_logit)


def solution(mesh):
    return jax.shard_map(
        body,
        mesh=mesh,
        in_specs=(
            P("seq", None),
            P(),
            P(),
            P(None, "tp"),
            P(None, "tp"),
            P(None, "tp"),
            P(None, "tp"),
            P(None, "tp"),
            P(None, "tp"),
            P("tp"),
            P("tp"),
            P(None, "tp"),
            P(None, "tp"),
            P(None, "tp"),
            P(),
            P("tp", None),
            P(),
            P(None, ("seq", "tp")),
        ),
        out_specs=(P("seq", "tp"), P("seq", "tp", None, None), P()),
        check_vma=False,
    )
```

profile of v0, /device:TPU:1, one launch (start us, length us, event | category | flops | bytes accessed | tf_op | source)
XLA Modules:
  0.0 931.8 jit_solution(14299696759197903953)
XLA Ops:
  51.5 133.2 %while.24 = (s32[]{:T(128)}, f32[4,128,384]{2,1,0:T(8,128)S(1)}, f32[4,4,64,384]{3,2,0,1:T(8,128)}, f32[4,4,128,384]{3,2,1,0:T(8,128)}, f32[4,4,64]{2,1,0:T(4,12...) while((s32[]{:T(128)}, f32[4,128,384]{2,1,0:T(8,128)S(1)}, ...), condition=%wide.region_8.9_spmd, body=%wide.region_7.8_spmd.sunk | while | flops 656073024 | bytes 11045709 | solution.py:145
  54.5 20.4 %custom-call.8 = f32[4,1,64,64]{2,3,1,0:T(8,128)S(1)} custom-call(f32[4,1,64,64]{3,2,1,0:T(8,128)} %fusion.136), custom_call_target="InvertDiagBlocksLowerTriangular" | custom-call | tf_op jit(solution)/shard_map/while/body/eval_jaxpr/triangular_solve | solution.py:62
  87.8 20.4 %custom-call.8 = f32[4,1,64,64]{2,3,1,0:T(8,128)S(1)} custom-call(f32[4,1,64,64]{3,2,1,0:T(8,128)} %fusion.136), custom_call_target="InvertDiagBlocksLowerTriangular" | custom-call | tf_op jit(solution)/shard_map/while/body/eval_jaxpr/triangular_solve | solution.py:62
  121.1 20.4 %custom-call.8 = f32[4,1,64,64]{2,3,1,0:T(8,128)S(1)} custom-call(f32[4,1,64,64]{3,2,1,0:T(8,128)} %fusion.136), custom_call_target="InvertDiagBlocksLowerTriangular" | custom-call | tf_op jit(solution)/shard_map/while/body/eval_jaxpr/triangular_solve | solution.py:62
  154.4 20.4 %custom-call.8 = f32[4,1,64,64]{2,3,1,0:T(8,128)S(1)} custom-call(f32[4,1,64,64]{3,2,1,0:T(8,128)} %fusion.136), custom_call_target="InvertDiagBlocksLowerTriangular" | custom-call | tf_op jit(solution)/shard_map/while/body/eval_jaxpr/triangular_solve | solution.py:62
  185.6 428.0 %while.25 = (s32[]{:T(128)}, f32[4,128,256]{2,1,0:T(8,128)S(1)}, f32[4,128,128]{2,1,0:T(8,128)}, f32[4,128,256]{2,1,0:T(8,128)S(1)}, s32[]{:T(128)}) while((s32[]{:T(128)}, f32[4,128,256]{2,1,0:T(8,128)S(1)}, f32[4,128,128]{2,1,0:T(8,128)}, f32[4,128,256]{2,1,0:T(8,128)S(1)}, s32[]{:T(128)}) %tuple.75), condition=%wide.region_10.11_spmd, body=%wide.region_9.10_spmd.sunk | while | flops 201457664 | bytes 3932261 | solution.py:155
  189.9 6.4 collective-permute-done
  202.9 6.4 collective-permute-done
  215.9 6.4 collective-permute-done
  228.9 6.4 collective-permute-done
  241.9 6.4 collective-permute-done
  255.0 6.4 collective-permute-done
  268.0 6.4 collective-permute-done
  281.0 6.4 collective-permute-done
  294.0 6.4 collective-permute-done
  307.1 6.4 collective-permute-done
  320.1 6.4 collective-permute-done
  333.1 6.4 collective-permute-done
  346.1 6.4 collective-permute-done
  359.2 6.4 collective-permute-done
  372.2 6.4 collective-permute-done
  398.2 6.4 collective-permute-done
  440.7 6.4 collective-permute-done
  471.0 6.4 collective-permute-done
  516.4 6.4 collective-permute-done
  546.7 6.4 collective-permute-done
  576.9 6.4 collective-permute-done
  592.1 6.4 collective-permute-done
  620.6 8.3 fusion.47
  637.6 89.2 %all-reduce.4.cloned.1.call-done = f32[256,2048]{1,0:T(8,128)} async-done(((f32[256,2048]{1,0:T(8,128)}), f32[256,2048]{1,0:T(8,128)}) %all-reduce.4.cloned.1.call-update) | async-done | bytes 2097168 | tf_op jit(solution)/shard_map/psum | solution.py:175
  729.2 123.1 %psum.15 = bf16[4,2048]{1,0:T(4,128)(2,1)S(1)} all-reduce(bf16[4,2048]{1,0:T(4,128)(2,1)S(1)} %convolution_convert_fusion), channel_id=1, replica_groups=mesh['seq'=32,'tp'=4] {'seq'}, use_global_device_ids=true, to_apply=%region_13.14 | all-reduce | flops 8192 | bytes 32768 | tf_op jit(solution)/shard_map/psum | solution.py:179
  857.0 67.2 %pmax.7 = f32[4]{0:T(128)} all-reduce(f32[4]{0:T(128)S(1)} %convolution_reduce_fusion), channel_id=1, replica_groups=mesh['seq'=32,'tp'=4] {'seq','tp'}, use_global_device_ids=true, to_apply=%region_16.17 | all-reduce | flops 4 | bytes 32 | tf_op jit(solution)/shard_map/pmax | solution.py:182
  (295 shorter events, 405.9 us)
Async XLA Ops:
  7.2 719.6 %all-reduce.4.cloned.1.call-start = ((), (), s32[]{:S(2)}) async-start(), calls=%async_computation | async-start | bytes 4194304 | tf_op jit(solution)/shard_map/psum | solution.py:175
  15.9 12.0 %collective-permute-start.1 = (bf16[3,2048]{1,0:T(4,128)(2,1)S(1)}, bf16[3,2048]{1,0:T(4,128)(2,1)S(1)}, u32[]{:S(2)}, u32[]{:S(2)}) collective-permute-start(bf16[3,2048]{1,0:T(4,128)(2,1)S(1)} %slice.76), channel_id=1, source_target_pairs={{0,4},{4,8},{8,12},{12,16},{16,20},{20,24},{24,28},{28,32},{32,36}... | collective-permute-start | bytes 36872 | tf_op jit(solution)/shard_map/ppermute | solution.py:15
  198.6 10.7 %collective-permute-start = (f32[4,128,256]{2,1,0:T(8,128)}, f32[4,128,256]{2,1,0:T(8,128)S(1)}, u32[]{:S(2)}, u32[]{:S(2)}) collective-permute-start(f32[4,128,256]{2,1,0:T(8,128)} %convolution_add_fusion.5), channel_id=1, source_target_pairs={{0,4},{4,8},{8,12},{12,16},{16,20},{20,24},{24,28},{28,32},{32,36}... | collective-permute-start | bytes 1572872 | tf_op jit(solution)/shard_map/while/body/eval_jaxpr/ppermute | solution.py:15
  211.6 10.7 %collective-permute-start = (f32[4,128,256]{2,1,0:T(8,128)}, f32[4,128,256]{2,1,0:T(8,128)S(1)}, u32[]{:S(2)}, u32[]{:S(2)}) collective-permute-start(f32[4,128,256]{2,1,0:T(8,128)} %convolution_add_fusion.5), channel_id=1, source_target_pairs={{0,4},{4,8},{8,12},{12,16},{16,20},{20,24},{24,28},{28,32},{32,36}... | collective-permute-start | bytes 1572872 | tf_op jit(solution)/shard_map/while/body/eval_jaxpr/ppermute | solution.py:15
  224.6 10.7 %collective-permute-start = (f32[4,128,256]{2,1,0:T(8,128)}, f32[4,128,256]{2,1,0:T(8,128)S(1)}, u32[]{:S(2)}, u32[]{:S(2)}) collective-permute-start(f32[4,128,256]{2,1,0:T(8,128)} %convolution_add_fusion.5), channel_id=1, source_target_pairs={{0,4},{4,8},{8,12},{12,16},{16,20},{20,24},{24,28},{28,32},{32,36}... | collective-permute-start | bytes 1572872 | tf_op jit(solution)/shard_map/while/body/eval_jaxpr/ppermute | solution.py:15
  237.7 10.7 %collective-permute-start = (f32[4,128,256]{2,1,0:T(8,128)}, f32[4,128,256]{2,1,0:T(8,128)S(1)}, u32[]{:S(2)}, u32[]{:S(2)}) collective-permute-start(f32[4,128,256]{2,1,0:T(8,128)} %convolution_add_fusion.5), channel_id=1, source_target_pairs={{0,4},{4,8},{8,12},{12,16},{16,20},{20,24},{24,28},{28,32},{32,36}... | collective-permute-start | bytes 1572872 | tf_op jit(solution)/shard_map/while/body/eval_jaxpr/ppermute | solution.py:15
  250.7 10.7 %collective-permute-start = (f32[4,128,256]{2,1,0:T(8,128)}, f32[4,128,256]{2,1,0:T(8,128)S(1)}, u32[]{:S(2)}, u32[]{:S(2)}) collective-permute-start(f32[4,128,256]{2,1,0:T(8,128)} %convolution_add_fusion.5), channel_id=1, source_target_pairs={{0,4},{4,8},{8,12},{12,16},{16,20},{20,24},{24,28},{28,32},{32,36}... | collective-permute-start | bytes 1572872 | tf_op jit(solution)/shard_map/while/body/eval_jaxpr/ppermute | solution.py:15
  263.7 10.7 %collective-permute-start = (f32[4,128,256]{2,1,0:T(8,128)}, f32[4,128,256]{2,1,0:T(8,128)S(1)}, u32[]{:S(2)}, u32[]{:S(2)}) collective-permute-start(f32[4,128,256]{2,1,0:T(8,128)} %convolution_add_fusion.5), channel_id=1, source_target_pairs={{0,4},{4,8},{8,12},{12,16},{16,20},{20,24},{24,28},{28,32},{32,36}... | collective-permute-start | bytes 1572872 | tf_op jit(solution)/shard_map/while/body/eval_jaxpr/ppermute | solution.py:15
  276.7 10.7 %collective-permute-start = (f32[4,128,256]{2,1,0:T(8,128)}, f32[4,128,256]{2,1,0:T(8,128)S(1)}, u32[]{:S(2)}, u32[]{:S(2)}) collective-permute-start(f32[4,128,256]{2,1,0:T(8,128)} %convolution_add_fusion.5), channel_id=1, source_target_pairs={{0,4},{4,8},{8,12},{12,16},{16,20},{20,24},{24,28},{28,32},{32,36}... | collective-permute-start | bytes 1572872 | tf_op jit(solution)/shard_map/while/body/eval_jaxpr/ppermute | solution.py:15
  289.8 10.7 %collective-permute-start = (f32[4,128,256]{2,1,0:T(8,128)}, f32[4,128,256]{2,1,0:T(8,128)S(1)}, u32[]{:S(2)}, u32[]{:S(2)}) collective-permute-start(f32[4,128,256]{2,1,0:T(8,128)} %convolution_add_fusion.5), channel_id=1, source_target_pairs={{0,4},{4,8},{8,12},{12,16},{16,20},{20,24},{24,28},{28,32},{32,36}... | collective-permute-start | bytes 1572872 | tf_op jit(solution)/shard_map/while/body/eval_jaxpr/ppermute | solution.py:15
  302.8 10.7 %collective-permute-start = (f32[4,128,256]{2,1,0:T(8,128)}, f32[4,128,256]{2,1,0:T(8,128)S(1)}, u32[]{:S(2)}, u32[]{:S(2)}) collective-permute-start(f32[4,128,256]{2,1,0:T(8,128)} %convolution_add_fusion.5), channel_id=1, source_target_pairs={{0,4},{4,8},{8,12},{12,16},{16,20},{20,24},{24,28},{28,32},{32,36}... | collective-permute-start | bytes 1572872 | tf_op jit(solution)/shard_map/while/body/eval_jaxpr/ppermute | solution.py:15
  315.8 10.7 %collective-permute-start = (f32[4,128,256]{2,1,0:T(8,128)}, f32[4,128,256]{2,1,0:T(8,128)S(1)}, u32[]{:S(2)}, u32[]{:S(2)}) collective-permute-start(f32[4,128,256]{2,1,0:T(8,128)} %convolution_add_fusion.5), channel_id=1, source_target_pairs={{0,4},{4,8},{8,12},{12,16},{16,20},{20,24},{24,28},{28,32},{32,36}... | collective-permute-start | bytes 1572872 | tf_op jit(solution)/shard_map/while/body/eval_jaxpr/ppermute | solution.py:15
  328.8 10.7 %collective-permute-start = (f32[4,128,256]{2,1,0:T(8,128)}, f32[4,128,256]{2,1,0:T(8,128)S(1)}, u32[]{:S(2)}, u32[]{:S(2)}) collective-permute-start(f32[4,128,256]{2,1,0:T(8,128)} %convolution_add_fusion.5), channel_id=1, source_target_pairs={{0,4},{4,8},{8,12},{12,16},{16,20},{20,24},{24,28},{28,32},{32,36}... | collective-permute-start | bytes 1572872 | tf_op jit(solution)/shard_map/while/body/eval_jaxpr/ppermute | solution.py:15
  341.9 10.7 %collective-permute-start = (f32[4,128,256]{2,1,0:T(8,128)}, f32[4,128,256]{2,1,0:T(8,128)S(1)}, u32[]{:S(2)}, u32[]{:S(2)}) collective-permute-start(f32[4,128,256]{2,1,0:T(8,128)} %convolution_add_fusion.5), channel_id=1, source_target_pairs={{0,4},{4,8},{8,12},{12,16},{16,20},{20,24},{24,28},{28,32},{32,36}... | collective-permute-start | bytes 1572872 | tf_op jit(solution)/shard_map/while/body/eval_jaxpr/ppermute | solution.py:15
  354.9 10.7 %collective-permute-start = (f32[4,128,256]{2,1,0:T(8,128)}, f32[4,128,256]{2,1,0:T(8,128)S(1)}, u32[]{:S(2)}, u32[]{:S(2)}) collective-permute-start(f32[4,128,256]{2,1,0:T(8,128)} %convolution_add_fusion.5), channel_id=1, source_target_pairs={{0,4},{4,8},{8,12},{12,16},{16,20},{20,24},{24,28},{28,32},{32,36}... | collective-permute-start | bytes 1572872 | tf_op jit(solution)/shard_map/while/body/eval_jaxpr/ppermute | solution.py:15
  367.9 10.7 %collective-permute-start = (f32[4,128,256]{2,1,0:T(8,128)}, f32[4,128,256]{2,1,0:T(8,128)S(1)}, u32[]{:S(2)}, u32[]{:S(2)}) collective-permute-start(f32[4,128,256]{2,1,0:T(8,128)} %convolution_add_fusion.5), channel_id=1, source_target_pairs={{0,4},{4,8},{8,12},{12,16},{16,20},{20,24},{24,28},{28,32},{32,36}... | collective-permute-start | bytes 1572872 | tf_op jit(solution)/shard_map/while/body/eval_jaxpr/ppermute | solution.py:15
  380.9 10.7 %collective-permute-start = (f32[4,128,256]{2,1,0:T(8,128)}, f32[4,128,256]{2,1,0:T(8,128)S(1)}, u32[]{:S(2)}, u32[]{:S(2)}) collective-permute-start(f32[4,128,256]{2,1,0:T(8,128)} %convolution_add_fusion.5), channel_id=1, source_target_pairs={{0,4},{4,8},{8,12},{12,16},{16,20},{20,24},{24,28},{28,32},{32,36}... | collective-permute-start | bytes 1572872 | tf_op jit(solution)/shard_map/while/body/eval_jaxpr/ppermute | solution.py:15
  394.0 10.7 %collective-permute-start = (f32[4,128,256]{2,1,0:T(8,128)}, f32[4,128,256]{2,1,0:T(8,128)S(1)}, u32[]{:S(2)}, u32[]{:S(2)}) collective-permute-start(f32[4,128,256]{2,1,0:T(8,128)} %convolution_add_fusion.5), channel_id=1, source_target_pairs={{0,4},{4,8},{8,12},{12,16},{16,20},{20,24},{24,28},{28,32},{32,36}... | collective-permute-start | bytes 1572872 | tf_op jit(solution)/shard_map/while/body/eval_jaxpr/ppermute | solution.py:15
  407.0 10.7 %collective-permute-start = (f32[4,128,256]{2,1,0:T(8,128)}, f32[4,128,256]{2,1,0:T(8,128)S(1)}, u32[]{:S(2)}, u32[]{:S(2)}) collective-permute-start(f32[4,128,256]{2,1,0:T(8,128)} %convolution_add_fusion.5), channel_id=1, source_target_pairs={{0,4},{4,8},{8,12},{12,16},{16,20},{20,24},{24,28},{28,32},{32,36}... | collective-permute-start | bytes 1572872 | tf_op jit(solution)/shard_map/while/body/eval_jaxpr/ppermute | solution.py:15
  420.0 12.0 %collective-permute-start = (f32[4,128,256]{2,1,0:T(8,128)}, f32[4,128,256]{2,1,0:T(8,128)S(1)}, u32[]{:S(2)}, u32[]{:S(2)}) collective-permute-start(f32[4,128,256]{2,1,0:T(8,128)} %convolution_add_fusion.5), channel_id=1, source_target_pairs={{0,4},{4,8},{8,12},{12,16},{16,20},{20,24},{24,28},{28,32},{32,36}... | collective-permute-start | bytes 1572872 | tf_op jit(solution)/shard_map/while/body/eval_jaxpr/ppermute | solution.py:15
  434.4 12.8 %collective-permute-start = (f32[4,128,256]{2,1,0:T(8,128)}, f32[4,128,256]{2,1,0:T(8,128)S(1)}, u32[]{:S(2)}, u32[]{:S(2)}) collective-permute-start(f32[4,128,256]{2,1,0:T(8,128)} %convolution_add_fusion.5), channel_id=1, source_target_pairs={{0,4},{4,8},{8,12},{12,16},{16,20},{20,24},{24,28},{28,32},{32,36}... | collective-permute-start | bytes 1572872 | tf_op jit(solution)/shard_map/while/body/eval_jaxpr/ppermute | solution.py:15
  449.5 12.8 %collective-permute-start = (f32[4,128,256]{2,1,0:T(8,128)}, f32[4,128,256]{2,1,0:T(8,128)S(1)}, u32[]{:S(2)}, u32[]{:S(2)}) collective-permute-start(f32[4,128,256]{2,1,0:T(8,128)} %convolution_add_fusion.5), channel_id=1, source_target_pairs={{0,4},{4,8},{8,12},{12,16},{16,20},{20,24},{24,28},{28,32},{32,36}... | collective-permute-start | bytes 1572872 | tf_op jit(solution)/shard_map/while/body/eval_jaxpr/ppermute | solution.py:15
  464.6 12.8 %collective-permute-start = (f32[4,128,256]{2,1,0:T(8,128)}, f32[4,128,256]{2,1,0:T(8,128)S(1)}, u32[]{:S(2)}, u32[]{:S(2)}) collective-permute-start(f32[4,128,256]{2,1,0:T(8,128)} %convolution_add_fusion.5), channel_id=1, source_target_pairs={{0,4},{4,8},{8,12},{12,16},{16,20},{20,24},{24,28},{28,32},{32,36}... | collective-permute-start | bytes 1572872 | tf_op jit(solution)/shard_map/while/body/eval_jaxpr/ppermute | solution.py:15
  479.7 12.8 %collective-permute-start = (f32[4,128,256]{2,1,0:T(8,128)}, f32[4,128,256]{2,1,0:T(8,128)S(1)}, u32[]{:S(2)}, u32[]{:S(2)}) collective-permute-start(f32[4,128,256]{2,1,0:T(8,128)} %convolution_add_fusion.5), channel_id=1, source_target_pairs={{0,4},{4,8},{8,12},{12,16},{16,20},{20,24},{24,28},{28,32},{32,36}... | collective-permute-start | bytes 1572872 | tf_op jit(solution)/shard_map/while/body/eval_jaxpr/ppermute | solution.py:15
  494.9 12.8 %collective-permute-start = (f32[4,128,256]{2,1,0:T(8,128)}, f32[4,128,256]{2,1,0:T(8,128)S(1)}, u32[]{:S(2)}, u32[]{:S(2)}) collective-permute-start(f32[4,128,256]{2,1,0:T(8,128)} %convolution_add_fusion.5), channel_id=1, source_target_pairs={{0,4},{4,8},{8,12},{12,16},{16,20},{20,24},{24,28},{28,32},{32,36}... | collective-permute-start | bytes 1572872 | tf_op jit(solution)/shard_map/while/body/eval_jaxpr/ppermute | solution.py:15
  510.0 12.8 %collective-permute-start = (f32[4,128,256]{2,1,0:T(8,128)}, f32[4,128,256]{2,1,0:T(8,128)S(1)}, u32[]{:S(2)}, u32[]{:S(2)}) collective-permute-start(f32[4,128,256]{2,1,0:T(8,128)} %convolution_add_fusion.5), channel_id=1, source_target_pairs={{0,4},{4,8},{8,12},{12,16},{16,20},{20,24},{24,28},{28,32},{32,36}... | collective-permute-start | bytes 1572872 | tf_op jit(solution)/shard_map/while/body/eval_jaxpr/ppermute | solution.py:15
  525.1 12.8 %collective-permute-start = (f32[4,128,256]{2,1,0:T(8,128)}, f32[4,128,256]{2,1,0:T(8,128)S(1)}, u32[]{:S(2)}, u32[]{:S(2)}) collective-permute-start(f32[4,128,256]{2,1,0:T(8,128)} %convolution_add_fusion.5), channel_id=1, source_target_pairs={{0,4},{4,8},{8,12},{12,16},{16,20},{20,24},{24,28},{28,32},{32,36}... | collective-permute-start | bytes 1572872 | tf_op jit(solution)/shard_map/while/body/eval_jaxpr/ppermute | solution.py:15
  540.3 12.8 %collective-permute-start = (f32[4,128,256]{2,1,0:T(8,128)}, f32[4,128,256]{2,1,0:T(8,128)S(1)}, u32[]{:S(2)}, u32[]{:S(2)}) collective-permute-start(f32[4,128,256]{2,1,0:T(8,128)} %convolution_add_fusion.5), channel_id=1, source_target_pairs={{0,4},{4,8},{8,12},{12,16},{16,20},{20,24},{24,28},{28,32},{32,36}... | collective-permute-start | bytes 1572872 | tf_op jit(solution)/shard_map/while/body/eval_jaxpr/ppermute | solution.py:15
  555.4 12.8 %collective-permute-start = (f32[4,128,256]{2,1,0:T(8,128)}, f32[4,128,256]{2,1,0:T(8,128)S(1)}, u32[]{:S(2)}, u32[]{:S(2)}) collective-permute-start(f32[4,128,256]{2,1,0:T(8,128)} %convolution_add_fusion.5), channel_id=1, source_target_pairs={{0,4},{4,8},{8,12},{12,16},{16,20},{20,24},{24,28},{28,32},{32,36}... | collective-permute-start | bytes 1572872 | tf_op jit(solution)/shard_map/while/body/eval_jaxpr/ppermute | solution.py:15
  570.5 12.8 %collective-permute-start = (f32[4,128,256]{2,1,0:T(8,128)}, f32[4,128,256]{2,1,0:T(8,128)S(1)}, u32[]{:S(2)}, u32[]{:S(2)}) collective-permute-start(f32[4,128,256]{2,1,0:T(8,128)} %convolution_add_fusion.5), channel_id=1, source_target_pairs={{0,4},{4,8},{8,12},{12,16},{16,20},{20,24},{24,28},{28,32},{32,36}... | collective-permute-start | bytes 1572872 | tf_op jit(solution)/shard_map/while/body/eval_jaxpr/ppermute | solution.py:15
  585.7 12.8 %collective-permute-start = (f32[4,128,256]{2,1,0:T(8,128)}, f32[4,128,256]{2,1,0:T(8,128)S(1)}, u32[]{:S(2)}, u32[]{:S(2)}) collective-permute-start(f32[4,128,256]{2,1,0:T(8,128)} %convolution_add_fusion.5), channel_id=1, source_target_pairs={{0,4},{4,8},{8,12},{12,16},{16,20},{20,24},{24,28},{28,32},{32,36}... | collective-permute-start | bytes 1572872 | tf_op jit(solution)/shard_map/while/body/eval_jaxpr/ppermute | solution.py:15
  600.8 12.8 %collective-permute-start = (f32[4,128,256]{2,1,0:T(8,128)}, f32[4,128,256]{2,1,0:T(8,128)S(1)}, u32[]{:S(2)}, u32[]{:S(2)}) collective-permute-start(f32[4,128,256]{2,1,0:T(8,128)} %convolution_add_fusion.5), channel_id=1, source_target_pairs={{0,4},{4,8},{8,12},{12,16},{16,20},{20,24},{24,28},{28,32},{32,36}... | collective-permute-start | bytes 1572872 | tf_op jit(solution)/shard_map/while/body/eval_jaxpr/ppermute | solution.py:15
  (41 other events, 462.0 us)
Sparse Core Ops, SparseCore 0:
  629.0 97.7 all-reduce.3
where the time goes:
time: 935 us; the launch traced here: 932 us
  waiting for transfers between devices  288 us (31%)
  blocking collectives  190 us (20%)
  starting transfers between devices  161 us (17%)
  matrix products  136 us (15%)
  other arithmetic  100 us (11%)
  local copies, waits for them, and re-layouts  40.7 us (4%)
  between operations  14.5 us (2%)
    ppermute x32, waiting for transfers between devices, from_behind(): lax.ppermute(value, axis, [(source, source + steps) for source in range(f...  199 us
    ppermute x32, starting transfers between devices, from_behind(): lax.ppermute(value, axis, [(source, source + steps) for source in range(f...  161 us
    psum x1, blocking collectives, body(): last_rows = lax.psum(picked.astype(jnp.bfloat16), 'seq').astype(jnp.float32)  123 us
    psum x1, waiting for transfers between devices, body(): summed = lax.psum(partial_out, 'tp')  89.2 us
    another operation x12, other arithmetic, block_step(): lax.linalg.triangular_solve(system_mat, right_side, left_side=True, lower...  81.6 us
    dot_general x31, matrix products, relay_turn(): jnp.einsum('hde,hef->hdf', lin_map, incoming, precision=HIGH) + offset_state  72.1 us
    pmax x1, blocking collectives, body(): max_logit = lax.pmax(jnp.max(logits, axis=1), ('seq', 'tp'))  67.2 us
  transfers between devices with their start and end apart: 33, of which 32 were waited for; matrix products, arithmetic and copies ran while one was open for 2% of the time, Pallas kernels for 0%

commit v1 on v0

--- a/solution.py
+++ b/solution.py
@@ -172,7 +172,9 @@
     col_start = lax.axis_index("tp") * share_cols
     last_tok = ends * BLOCK_LEN - 1
     picker = (last_tok[:, None] == positions[None, :]).astype(jnp.bfloat16)
-    summed = lax.psum(partial_out, "tp")
+    summed = partial_out
+    for hop in (1, 2):
+        summed = summed + lax.ppermute(summed, "tp", [(dev, dev ^ hop) for dev in range(4)])
     hidden_full = (x_float + summed).astype(jnp.bfloat16)
     hidden = lax.dynamic_slice_in_dim(hidden_full, col_start, share_cols, 1)
     picked = jnp.dot(picker, hidden_full, preferred_element_type=jnp.float32)

time: 935 us -> 932 us (level)
  waiting for transfers between devices: 288 us -> 267 us
  blocking collectives: 190 us -> 210 us
  between operations: 14.5 us -> 1.13 us
    psum x1 -> x0, waiting for transfers between devices: 89.2 us -> none  [body(): summed = lax.psum(partial_out, 'tp')]
    ppermute x0 -> x2, waiting for transfers between devices: none -> 68.3 us  [body(): lax.ppermute(summed, 'tp', [(dev, dev ^ hop) for dev in range(4)])]
    psum x1, blocking collectives: 123 us -> 143 us  [body(): last_rows = lax.psum(picked.astype(jnp.bfloat16), 'seq').astype(jnp.float32)]
  transfers between devices with their start and end apart: 33 -> 34, of which waited for: 32 -> 33; matrix products, arithmetic and copies ran while one was open for 2% -> 2% of each run, Pallas kernels for 0% -> 0%
where the time goes in v1:
time: 932 us; the launch traced here: 929 us
  waiting for transfers between devices  267 us (29%)
  blocking collectives  210 us (23%)
  starting transfers between devices  169 us (18%)
  matrix products  136 us (15%)
  other arithmetic  104 us (11%)
  local copies, waits for them, and re-layouts  40.9 us (4%)
    ppermute x32, waiting for transfers between devices, from_behind(): lax.ppermute(value, axis, [(source, source + steps) for source in range(f...  199 us
    ppermute x32, starting transfers between devices, from_behind(): lax.ppermute(value, axis, [(source, source + steps) for source in range(f...  161 us
    psum x1, blocking collectives, body(): last_rows = lax.psum(picked.astype(jnp.bfloat16), 'seq').astype(jnp.float32)  143 us
    another operation x12, other arithmetic, block_step(): lax.linalg.triangular_solve(system_mat, right_side, left_side=True, lower...  81.6 us
    dot_general x31, matrix products, relay_turn(): jnp.einsum('hde,hef->hdf', lin_map, incoming, precision=HIGH) + offset_state  72.2 us
    ppermute x2, waiting for transfers between devices, body(): lax.ppermute(summed, 'tp', [(dev, dev ^ hop) for dev in range(4)])  68.3 us
    pmax x1, blocking collectives, body(): max_logit = lax.pmax(jnp.max(logits, axis=1), ('seq', 'tp'))  67 us
  transfers between devices with their start and end apart: 34, of which 33 were waited for; matrix products, arithmetic and copies ran while one was open for 2% of the time, Pallas kernels for 0%

profile of v1, /device:TPU:1, one launch (start us, length us, event | category | flops | bytes accessed | tf_op | source)
XLA Modules:
  0.0 928.7 jit_solution(3219947116932464309)
XLA Ops:
  44.9 133.5 %while.24 = (s32[]{:T(128)}, f32[4,128,384]{2,1,0:T(8,128)S(1)}, f32[4,4,64,384]{3,2,0,1:T(8,128)}, f32[4,4,128,384]{3,2,1,0:T(8,128)}, f32[4,4,64]{2,1,0:T(4,12...) while((s32[]{:T(128)}, f32[4,128,384]{2,1,0:T(8,128)S(1)}, ...), condition=%wide.region_8.9_spmd, body=%wide.region_7.8_spmd.sunk | while | flops 656073024 | bytes 11045709 | solution.py:145
  47.9 20.4 %custom-call.8 = f32[4,1,64,64]{2,3,1,0:T(8,128)S(1)} custom-call(f32[4,1,64,64]{3,2,1,0:T(8,128)} %fusion.136), custom_call_target="InvertDiagBlocksLowerTriangular" | custom-call | tf_op jit(solution)/shard_map/while/body/eval_jaxpr/triangular_solve | solution.py:62
  81.3 20.4 %custom-call.8 = f32[4,1,64,64]{2,3,1,0:T(8,128)S(1)} custom-call(f32[4,1,64,64]{3,2,1,0:T(8,128)} %fusion.136), custom_call_target="InvertDiagBlocksLowerTriangular" | custom-call | tf_op jit(solution)/shard_map/while/body/eval_jaxpr/triangular_solve | solution.py:62
  114.6 20.4 %custom-call.8 = f32[4,1,64,64]{2,3,1,0:T(8,128)S(1)} custom-call(f32[4,1,64,64]{3,2,1,0:T(8,128)} %fusion.136), custom_call_target="InvertDiagBlocksLowerTriangular" | custom-call | tf_op jit(solution)/shard_map/while/body/eval_jaxpr/triangular_solve | solution.py:62
  148.0 20.4 %custom-call.8 = f32[4,1,64,64]{2,3,1,0:T(8,128)S(1)} custom-call(f32[4,1,64,64]{3,2,1,0:T(8,128)} %fusion.136), custom_call_target="InvertDiagBlocksLowerTriangular" | custom-call | tf_op jit(solution)/shard_map/while/body/eval_jaxpr/triangular_solve | solution.py:62
  179.2 428.2 %while.25 = (s32[]{:T(128)}, f32[4,128,256]{2,1,0:T(8,128)S(1)}, f32[4,128,128]{2,1,0:T(8,128)}, f32[4,128,256]{2,1,0:T(8,128)S(1)}, s32[]{:T(128)}) while((s32[]{:T(128)}, f32[4,128,256]{2,1,0:T(8,128)S(1)}, f32[4,128,128]{2,1,0:T(8,128)}, f32[4,128,256]{2,1,0:T(8,128)S(1)}, s32[]{:T(128)}) %tuple.75), condition=%wide.region_10.11_spmd, body=%wide.region_9.10_spmd.sunk | while | flops 201457664 | bytes 3932261 | solution.py:155
  183.5 6.4 collective-permute-done
  196.5 6.4 collective-permute-done
  209.5 6.4 collective-permute-done
  222.6 6.4 collective-permute-done
  235.6 6.4 collective-permute-done
  248.6 6.4 collective-permute-done
  261.6 6.4 collective-permute-done
  274.7 6.4 collective-permute-done
  287.7 6.4 collective-permute-done
  300.7 6.4 collective-permute-done
  313.7 6.4 collective-permute-done
  326.8 6.4 collective-permute-done
  339.8 6.4 collective-permute-done
  352.8 6.4 collective-permute-done
  365.9 6.4 collective-permute-done
  378.9 6.4 collective-permute-done
  391.9 6.4 collective-permute-done
  479.9 6.4 collective-permute-done
  495.0 6.4 collective-permute-done
  510.1 6.4 collective-permute-done
  525.3 6.4 collective-permute-done
  614.3 8.3 fusion.47
  624.2 37.7 %collective-permute-done.2 = f32[256,2048]{1,0:T(8,128)S(1)} collective-permute-done((f32[256,2048]{1,0:T(8,128)}, f32[256,2048]{1,0:T(8,128)S(1)}, u32[]{:S(2)}, u32[]{:S(2)}) %collective-permute-start.2) | collective-permute-done | bytes 2097184 | tf_op jit(solution)/shard_map/ppermute | solution.py:177
  679.9 30.5 %collective-permute-done.3 = f32[256,2048]{1,0:T(8,128)} collective-permute-done((f32[256,2048]{1,0:T(8,128)}, f32[256,2048]{1,0:T(8,128)}, u32[]{:S(2)}, u32[]{:S(2)}) %collective-permute-start.3) | collective-permute-done | bytes 2097184 | tf_op jit(solution)/shard_map/ppermute | solution.py:177
  713.5 142.9 %psum.7 = bf16[4,2048]{1,0:T(4,128)(2,1)S(1)} all-reduce(bf16[4,2048]{1,0:T(4,128)(2,1)S(1)} %convolution_convert_fusion), channel_id=1, replica_groups=mesh['seq'=32,'tp'=4] {'seq'}, use_global_device_ids=true, to_apply=%region_12.13 | all-reduce | flops 8192 | bytes 32768 | tf_op jit(solution)/shard_map/psum | solution.py:181
  861.0 67.0 %pmax.7 = f32[4]{0:T(128)} all-reduce(f32[4]{0:T(128)S(1)} %convolution_reduce_fusion), channel_id=1, replica_groups=mesh['seq'=32,'tp'=4] {'seq','tp'}, use_global_device_ids=true, to_apply=%region_15.16 | all-reduce | flops 4 | bytes 32 | tf_op jit(solution)/shard_map/pmax | solution.py:184
  (299 shorter events, 424.2 us)
Async XLA Ops:
  9.4 12.0 %collective-permute-start.1 = (bf16[3,2048]{1,0:T(4,128)(2,1)S(1)}, bf16[3,2048]{1,0:T(4,128)(2,1)S(1)}, u32[]{:S(2)}, u32[]{:S(2)}) collective-permute-start(bf16[3,2048]{1,0:T(4,128)(2,1)S(1)} %slice.76), channel_id=1, source_target_pairs={{0,4},{4,8},{8,12},{12,16},{16,20},{20,24},{24,28},{28,32},{32,36}... | collective-permute-start | bytes 36872 | tf_op jit(solution)/shard_map/ppermute | solution.py:15
  192.2 10.7 %collective-permute-start = (f32[4,128,256]{2,1,0:T(8,128)}, f32[4,128,256]{2,1,0:T(8,128)S(1)}, u32[]{:S(2)}, u32[]{:S(2)}) collective-permute-start(f32[4,128,256]{2,1,0:T(8,128)} %convolution_add_fusion.5), channel_id=1, source_target_pairs={{0,4},{4,8},{8,12},{12,16},{16,20},{20,24},{24,28},{28,32},{32,36}... | collective-permute-start | bytes 1572872 | tf_op jit(solution)/shard_map/while/body/eval_jaxpr/ppermute | solution.py:15
  205.2 10.7 %collective-permute-start = (f32[4,128,256]{2,1,0:T(8,128)}, f32[4,128,256]{2,1,0:T(8,128)S(1)}, u32[]{:S(2)}, u32[]{:S(2)}) collective-permute-start(f32[4,128,256]{2,1,0:T(8,128)} %convolution_add_fusion.5), channel_id=1, source_target_pairs={{0,4},{4,8},{8,12},{12,16},{16,20},{20,24},{24,28},{28,32},{32,36}... | collective-permute-start | bytes 1572872 | tf_op jit(solution)/shard_map/while/body/eval_jaxpr/ppermute | solution.py:15
  218.3 10.7 %collective-permute-start = (f32[4,128,256]{2,1,0:T(8,128)}, f32[4,128,256]{2,1,0:T(8,128)S(1)}, u32[]{:S(2)}, u32[]{:S(2)}) collective-permute-start(f32[4,128,256]{2,1,0:T(8,128)} %convolution_add_fusion.5), channel_id=1, source_target_pairs={{0,4},{4,8},{8,12},{12,16},{16,20},{20,24},{24,28},{28,32},{32,36}... | collective-permute-start | bytes 1572872 | tf_op jit(solution)/shard_map/while/body/eval_jaxpr/ppermute | solution.py:15
  231.3 10.7 %collective-permute-start = (f32[4,128,256]{2,1,0:T(8,128)}, f32[4,128,256]{2,1,0:T(8,128)S(1)}, u32[]{:S(2)}, u32[]{:S(2)}) collective-permute-start(f32[4,128,256]{2,1,0:T(8,128)} %convolution_add_fusion.5), channel_id=1, source_target_pairs={{0,4},{4,8},{8,12},{12,16},{16,20},{20,24},{24,28},{28,32},{32,36}... | collective-permute-start | bytes 1572872 | tf_op jit(solution)/shard_map/while/body/eval_jaxpr/ppermute | solution.py:15
  244.3 10.7 %collective-permute-start = (f32[4,128,256]{2,1,0:T(8,128)}, f32[4,128,256]{2,1,0:T(8,128)S(1)}, u32[]{:S(2)}, u32[]{:S(2)}) collective-permute-start(f32[4,128,256]{2,1,0:T(8,128)} %convolution_add_fusion.5), channel_id=1, source_target_pairs={{0,4},{4,8},{8,12},{12,16},{16,20},{20,24},{24,28},{28,32},{32,36}... | collective-permute-start | bytes 1572872 | tf_op jit(solution)/shard_map/while/body/eval_jaxpr/ppermute | solution.py:15
  257.4 10.7 %collective-permute-start = (f32[4,128,256]{2,1,0:T(8,128)}, f32[4,128,256]{2,1,0:T(8,128)S(1)}, u32[]{:S(2)}, u32[]{:S(2)}) collective-permute-start(f32[4,128,256]{2,1,0:T(8,128)} %convolution_add_fusion.5), channel_id=1, source_target_pairs={{0,4},{4,8},{8,12},{12,16},{16,20},{20,24},{24,28},{28,32},{32,36}... | collective-permute-start | bytes 1572872 | tf_op jit(solution)/shard_map/while/body/eval_jaxpr/ppermute | solution.py:15
  270.4 10.7 %collective-permute-start = (f32[4,128,256]{2,1,0:T(8,128)}, f32[4,128,256]{2,1,0:T(8,128)S(1)}, u32[]{:S(2)}, u32[]{:S(2)}) collective-permute-start(f32[4,128,256]{2,1,0:T(8,128)} %convolution_add_fusion.5), channel_id=1, source_target_pairs={{0,4},{4,8},{8,12},{12,16},{16,20},{20,24},{24,28},{28,32},{32,36}... | collective-permute-start | bytes 1572872 | tf_op jit(solution)/shard_map/while/body/eval_jaxpr/ppermute | solution.py:15
  283.4 10.7 %collective-permute-start = (f32[4,128,256]{2,1,0:T(8,128)}, f32[4,128,256]{2,1,0:T(8,128)S(1)}, u32[]{:S(2)}, u32[]{:S(2)}) collective-permute-start(f32[4,128,256]{2,1,0:T(8,128)} %convolution_add_fusion.5), channel_id=1, source_target_pairs={{0,4},{4,8},{8,12},{12,16},{16,20},{20,24},{24,28},{28,32},{32,36}... | collective-permute-start | bytes 1572872 | tf_op jit(solution)/shard_map/while/body/eval_jaxpr/ppermute | solution.py:15
  296.4 10.7 %collective-permute-start = (f32[4,128,256]{2,1,0:T(8,128)}, f32[4,128,256]{2,1,0:T(8,128)S(1)}, u32[]{:S(2)}, u32[]{:S(2)}) collective-permute-start(f32[4,128,256]{2,1,0:T(8,128)} %convolution_add_fusion.5), channel_id=1, source_target_pairs={{0,4},{4,8},{8,12},{12,16},{16,20},{20,24},{24,28},{28,32},{32,36}... | collective-permute-start | bytes 1572872 | tf_op jit(solution)/shard_map/while/body/eval_jaxpr/ppermute | solution.py:15
  309.5 10.7 %collective-permute-start = (f32[4,128,256]{2,1,0:T(8,128)}, f32[4,128,256]{2,1,0:T(8,128)S(1)}, u32[]{:S(2)}, u32[]{:S(2)}) collective-permute-start(f32[4,128,256]{2,1,0:T(8,128)} %convolution_add_fusion.5), channel_id=1, source_target_pairs={{0,4},{4,8},{8,12},{12,16},{16,20},{20,24},{24,28},{28,32},{32,36}... | collective-permute-start | bytes 1572872 | tf_op jit(solution)/shard_map/while/body/eval_jaxpr/ppermute | solution.py:15
  322.5 10.7 %collective-permute-start = (f32[4,128,256]{2,1,0:T(8,128)}, f32[4,128,256]{2,1,0:T(8,128)S(1)}, u32[]{:S(2)}, u32[]{:S(2)}) collective-permute-start(f32[4,128,256]{2,1,0:T(8,128)} %convolution_add_fusion.5), channel_id=1, source_target_pairs={{0,4},{4,8},{8,12},{12,16},{16,20},{20,24},{24,28},{28,32},{32,36}... | collective-permute-start | bytes 1572872 | tf_op jit(solution)/shard_map/while/body/eval_jaxpr/ppermute | solution.py:15
  335.5 10.7 %collective-permute-start = (f32[4,128,256]{2,1,0:T(8,128)}, f32[4,128,256]{2,1,0:T(8,128)S(1)}, u32[]{:S(2)}, u32[]{:S(2)}) collective-permute-start(f32[4,128,256]{2,1,0:T(8,128)} %convolution_add_fusion.5), channel_id=1, source_target_pairs={{0,4},{4,8},{8,12},{12,16},{16,20},{20,24},{24,28},{28,32},{32,36}... | collective-permute-start | bytes 1572872 | tf_op jit(solution)/shard_map/while/body/eval_jaxpr/ppermute | solution.py:15
  348.5 10.7 %collective-permute-start = (f32[4,128,256]{2,1,0:T(8,128)}, f32[4,128,256]{2,1,0:T(8,128)S(1)}, u32[]{:S(2)}, u32[]{:S(2)}) collective-permute-start(f32[4,128,256]{2,1,0:T(8,128)} %convolution_add_fusion.5), channel_id=1, source_target_pairs={{0,4},{4,8},{8,12},{12,16},{16,20},{20,24},{24,28},{28,32},{32,36}... | collective-permute-start | bytes 1572872 | tf_op jit(solution)/shard_map/while/body/eval_jaxpr/ppermute | solution.py:15
  361.6 10.7 %collective-permute-start = (f32[4,128,256]{2,1,0:T(8,128)}, f32[4,128,256]{2,1,0:T(8,128)S(1)}, u32[]{:S(2)}, u32[]{:S(2)}) collective-permute-start(f32[4,128,256]{2,1,0:T(8,128)} %convolution_add_fusion.5), channel_id=1, source_target_pairs={{0,4},{4,8},{8,12},{12,16},{16,20},{20,24},{24,28},{28,32},{32,36}... | collective-permute-start | bytes 1572872 | tf_op jit(solution)/shard_map/while/body/eval_jaxpr/ppermute | solution.py:15
  374.6 10.7 %collective-permute-start = (f32[4,128,256]{2,1,0:T(8,128)}, f32[4,128,256]{2,1,0:T(8,128)S(1)}, u32[]{:S(2)}, u32[]{:S(2)}) collective-permute-start(f32[4,128,256]{2,1,0:T(8,128)} %convolution_add_fusion.5), channel_id=1, source_target_pairs={{0,4},{4,8},{8,12},{12,16},{16,20},{20,24},{24,28},{28,32},{32,36}... | collective-permute-start | bytes 1572872 | tf_op jit(solution)/shard_map/while/body/eval_jaxpr/ppermute | solution.py:15
  387.6 10.7 %collective-permute-start = (f32[4,128,256]{2,1,0:T(8,128)}, f32[4,128,256]{2,1,0:T(8,128)S(1)}, u32[]{:S(2)}, u32[]{:S(2)}) collective-permute-start(f32[4,128,256]{2,1,0:T(8,128)} %convolution_add_fusion.5), channel_id=1, source_target_pairs={{0,4},{4,8},{8,12},{12,16},{16,20},{20,24},{24,28},{28,32},{32,36}... | collective-permute-start | bytes 1572872 | tf_op jit(solution)/shard_map/while/body/eval_jaxpr/ppermute | solution.py:15
  413.7 12.0 %collective-permute-start = (f32[4,128,256]{2,1,0:T(8,128)}, f32[4,128,256]{2,1,0:T(8,128)S(1)}, u32[]{:S(2)}, u32[]{:S(2)}) collective-permute-start(f32[4,128,256]{2,1,0:T(8,128)} %convolution_add_fusion.5), channel_id=1, source_target_pairs={{0,4},{4,8},{8,12},{12,16},{16,20},{20,24},{24,28},{28,32},{32,36}... | collective-permute-start | bytes 1572872 | tf_op jit(solution)/shard_map/while/body/eval_jaxpr/ppermute | solution.py:15
  428.1 12.8 %collective-permute-start = (f32[4,128,256]{2,1,0:T(8,128)}, f32[4,128,256]{2,1,0:T(8,128)S(1)}, u32[]{:S(2)}, u32[]{:S(2)}) collective-permute-start(f32[4,128,256]{2,1,0:T(8,128)} %convolution_add_fusion.5), channel_id=1, source_target_pairs={{0,4},{4,8},{8,12},{12,16},{16,20},{20,24},{24,28},{28,32},{32,36}... | collective-permute-start | bytes 1572872 | tf_op jit(solution)/shard_map/while/body/eval_jaxpr/ppermute | solution.py:15
  443.2 12.8 %collective-permute-start = (f32[4,128,256]{2,1,0:T(8,128)}, f32[4,128,256]{2,1,0:T(8,128)S(1)}, u32[]{:S(2)}, u32[]{:S(2)}) collective-permute-start(f32[4,128,256]{2,1,0:T(8,128)} %convolution_add_fusion.5), channel_id=1, source_target_pairs={{0,4},{4,8},{8,12},{12,16},{16,20},{20,24},{24,28},{28,32},{32,36}... | collective-permute-start | bytes 1572872 | tf_op jit(solution)/shard_map/while/body/eval_jaxpr/ppermute | solution.py:15
  458.3 12.8 %collective-permute-start = (f32[4,128,256]{2,1,0:T(8,128)}, f32[4,128,256]{2,1,0:T(8,128)S(1)}, u32[]{:S(2)}, u32[]{:S(2)}) collective-permute-start(f32[4,128,256]{2,1,0:T(8,128)} %convolution_add_fusion.5), channel_id=1, source_target_pairs={{0,4},{4,8},{8,12},{12,16},{16,20},{20,24},{24,28},{28,32},{32,36}... | collective-permute-start | bytes 1572872 | tf_op jit(solution)/shard_map/while/body/eval_jaxpr/ppermute | solution.py:15
  473.5 12.8 %collective-permute-start = (f32[4,128,256]{2,1,0:T(8,128)}, f32[4,128,256]{2,1,0:T(8,128)S(1)}, u32[]{:S(2)}, u32[]{:S(2)}) collective-permute-start(f32[4,128,256]{2,1,0:T(8,128)} %convolution_add_fusion.5), channel_id=1, source_target_pairs={{0,4},{4,8},{8,12},{12,16},{16,20},{20,24},{24,28},{28,32},{32,36}... | collective-permute-start | bytes 1572872 | tf_op jit(solution)/shard_map/while/body/eval_jaxpr/ppermute | solution.py:15
  488.6 12.8 %collective-permute-start = (f32[4,128,256]{2,1,0:T(8,128)}, f32[4,128,256]{2,1,0:T(8,128)S(1)}, u32[]{:S(2)}, u32[]{:S(2)}) collective-permute-start(f32[4,128,256]{2,1,0:T(8,128)} %convolution_add_fusion.5), channel_id=1, source_target_pairs={{0,4},{4,8},{8,12},{12,16},{16,20},{20,24},{24,28},{28,32},{32,36}... | collective-permute-start | bytes 1572872 | tf_op jit(solution)/shard_map/while/body/eval_jaxpr/ppermute | solution.py:15
  503.7 12.8 %collective-permute-start = (f32[4,128,256]{2,1,0:T(8,128)}, f32[4,128,256]{2,1,0:T(8,128)S(1)}, u32[]{:S(2)}, u32[]{:S(2)}) collective-permute-start(f32[4,128,256]{2,1,0:T(8,128)} %convolution_add_fusion.5), channel_id=1, source_target_pairs={{0,4},{4,8},{8,12},{12,16},{16,20},{20,24},{24,28},{28,32},{32,36}... | collective-permute-start | bytes 1572872 | tf_op jit(solution)/shard_map/while/body/eval_jaxpr/ppermute | solution.py:15
  518.9 12.8 %collective-permute-start = (f32[4,128,256]{2,1,0:T(8,128)}, f32[4,128,256]{2,1,0:T(8,128)S(1)}, u32[]{:S(2)}, u32[]{:S(2)}) collective-permute-start(f32[4,128,256]{2,1,0:T(8,128)} %convolution_add_fusion.5), channel_id=1, source_target_pairs={{0,4},{4,8},{8,12},{12,16},{16,20},{20,24},{24,28},{28,32},{32,36}... | collective-permute-start | bytes 1572872 | tf_op jit(solution)/shard_map/while/body/eval_jaxpr/ppermute | solution.py:15
  534.0 12.8 %collective-permute-start = (f32[4,128,256]{2,1,0:T(8,128)}, f32[4,128,256]{2,1,0:T(8,128)S(1)}, u32[]{:S(2)}, u32[]{:S(2)}) collective-permute-start(f32[4,128,256]{2,1,0:T(8,128)} %convolution_add_fusion.5), channel_id=1, source_target_pairs={{0,4},{4,8},{8,12},{12,16},{16,20},{20,24},{24,28},{28,32},{32,36}... | collective-permute-start | bytes 1572872 | tf_op jit(solution)/shard_map/while/body/eval_jaxpr/ppermute | solution.py:15
  549.1 12.8 %collective-permute-start = (f32[4,128,256]{2,1,0:T(8,128)}, f32[4,128,256]{2,1,0:T(8,128)S(1)}, u32[]{:S(2)}, u32[]{:S(2)}) collective-permute-start(f32[4,128,256]{2,1,0:T(8,128)} %convolution_add_fusion.5), channel_id=1, source_target_pairs={{0,4},{4,8},{8,12},{12,16},{16,20},{20,24},{24,28},{28,32},{32,36}... | collective-permute-start | bytes 1572872 | tf_op jit(solution)/shard_map/while/body/eval_jaxpr/ppermute | solution.py:15
  564.3 12.8 %collective-permute-start = (f32[4,128,256]{2,1,0:T(8,128)}, f32[4,128,256]{2,1,0:T(8,128)S(1)}, u32[]{:S(2)}, u32[]{:S(2)}) collective-permute-start(f32[4,128,256]{2,1,0:T(8,128)} %convolution_add_fusion.5), channel_id=1, source_target_pairs={{0,4},{4,8},{8,12},{12,16},{16,20},{20,24},{24,28},{28,32},{32,36}... | collective-permute-start | bytes 1572872 | tf_op jit(solution)/shard_map/while/body/eval_jaxpr/ppermute | solution.py:15
  579.4 12.8 %collective-permute-start = (f32[4,128,256]{2,1,0:T(8,128)}, f32[4,128,256]{2,1,0:T(8,128)S(1)}, u32[]{:S(2)}, u32[]{:S(2)}) collective-permute-start(f32[4,128,256]{2,1,0:T(8,128)} %convolution_add_fusion.5), channel_id=1, source_target_pairs={{0,4},{4,8},{8,12},{12,16},{16,20},{20,24},{24,28},{28,32},{32,36}... | collective-permute-start | bytes 1572872 | tf_op jit(solution)/shard_map/while/body/eval_jaxpr/ppermute | solution.py:15
  594.6 12.8 %collective-permute-start = (f32[4,128,256]{2,1,0:T(8,128)}, f32[4,128,256]{2,1,0:T(8,128)S(1)}, u32[]{:S(2)}, u32[]{:S(2)}) collective-permute-start(f32[4,128,256]{2,1,0:T(8,128)} %convolution_add_fusion.5), channel_id=1, source_target_pairs={{0,4},{4,8},{8,12},{12,16},{16,20},{20,24},{24,28},{28,32},{32,36}... | collective-permute-start | bytes 1572872 | tf_op jit(solution)/shard_map/while/body/eval_jaxpr/ppermute | solution.py:15
  622.6 39.4 %collective-permute-start.2 = (f32[256,2048]{1,0:T(8,128)}, f32[256,2048]{1,0:T(8,128)S(1)}, u32[]{:S(2)}, u32[]{:S(2)}) collective-permute-start(f32[256,2048]{1,0:T(8,128)} %fusion.47), channel_id=1, source_target_pairs={{0,1},{1,0},{2,3},{3,2},{4,5},{5,4},{6,7},{7,6},{8,9},{9,8},{10,11... | collective-permute-start | bytes 6291464 | tf_op jit(solution)/shard_map/ppermute | solution.py:177
  665.1 45.3 %collective-permute-start.3 = (f32[256,2048]{1,0:T(8,128)}, f32[256,2048]{1,0:T(8,128)}, u32[]{:S(2)}, u32[]{:S(2)}) collective-permute-start(f32[256,2048]{1,0:T(8,128)} %add.210), channel_id=1, source_target_pairs={{0,2},{1,3},{2,0},{3,1},{4,6},{5,7},{6,4},{7,5},{8,10},{9,11},{10,... | collective-permute-start | bytes 6291464 | tf_op jit(solution)/shard_map/ppermute | solution.py:177
  (43 other events, 412.7 us)
